TPU v7x, 32 devices: a whole 2x2x4 slice. The times are simulated.
32 devices in a mesh: groups: 2 (over x), hist: 8 (over z, y), users: 2 (over core).
Axes of the slice: x: 2, y: 2, z: 4, core: 2. Of those that a mesh axis runs over, the one named last changes fastest.
Arguments:
- targets: bfloat16 [4, 512, 1024], P(('groups', 'users'), 'hist'), parts along dimension 0, may hold values from -6 to 6
- hist_keys: bfloat16 [2, 4, 12288, 1024], P(None, ('groups', 'users'), 'hist'), parts along dimension 1, may hold values from -6 to 6
- hist_values: bfloat16 [2, 4, 12288, 1024], P(None, ('groups', 'users'), 'hist'), parts along dimension 1, may hold values from -6 to 6
- lengths: int32 [4], P(('groups', 'users')), parts along dimension 0, may hold values from 3072 to 12288
- cuts: int32 [4, 512], P(('groups', 'users')), parts along dimension 0, may hold values from 1 to 12288
- w_query: bfloat16 [2, 1024, 1024], replicated, may hold values from -0.1875 to 0.1875
- w_gate: bfloat16 [2, 1024, 1024], replicated, may hold values from -0.1875 to 0.1875
- w_out: bfloat16 [2, 1024, 1024], replicated, may hold values from -0.1875 to 0.1875
- ln_gain: float32 [2, 1024], replicated, may hold values from 0.1 to 1.9
Outputs:
- refined: bfloat16 [4, 512, 1024], P(('groups', 'users'), 'hist'), parts along dimension 0
There are 2 independent parts, one for each index of `groups`. A program takes and returns all parts, laid end to end along the dimension named above; an argument that names none is the same for every part. Nothing has to cross between parts.
All inputs are finite; a program needn't handle non-finite values.
Results may differ from a plain program's by a relative error of at most 0.012.
Values may be sent and summed in bfloat16 or wider, within the bound.
A program may use at most 128 MiB of HBM per device.

v0:
```python
import math

import jax
import jax.numpy as jnp
from jax import lax
from jax.sharding import PartitionSpec as P

D = 1024
HEADS = 8
LAYERS = 2


def attend_rows(queries, key_slab, value_slab, limits):
    row_count = queries.shape[0]
    hist_rows = key_slab.shape[0]
    head_size = D // HEADS
    factor = 1.0 / math.sqrt(head_size)
    query_heads = queries.reshape(row_count, HEADS, head_size)
    key_heads = key_slab.reshape(hist_rows, HEADS, head_size)
    value_heads = value_slab.reshape(hist_rows, HEADS, head_size)
    scores = (
        jnp.einsum("rhd,jhd->hrj", query_heads, key_heads, preferred_element_type=jnp.float32)
        * factor
    )
    positions = lax.broadcasted_iota(jnp.int32, (1, row_count, hist_rows), 2)
    visible = positions < limits[None, :, None]
    weights = jnp.where(visible, jax.nn.silu(scores), 0.0).astype(jnp.bfloat16)
    output = jnp.einsum("hrj,jhd->rhd", weights, value_heads, preferred_element_type=jnp.float32)
    return output.reshape(row_count, D)


def finish(hidden, summed, gating, out_weight, gain_row):
    centre = jnp.mean(summed, axis=-1, keepdims=True)
    spread = jnp.mean(jnp.square(summed - centre), axis=-1, keepdims=True)
    normed = ((summed - centre) * lax.rsqrt(spread + 1e-05) * gain_row * gating).astype(
        jnp.bfloat16
    )
    update = jnp.dot(normed, out_weight, preferred_element_type=jnp.float32)
    return (hidden.astype(jnp.float32) + update).astype(jnp.bfloat16)


def per_device(targets, hist_keys, hist_values, lengths, cuts, w_query, w_gate, w_out, ln_gain):
    hist_rows = hist_keys.shape[2]
    offset = lax.axis_index("hist") * hist_rows
    limits = jnp.minimum(cuts[0], lengths[0]) - offset
    hidden = targets[0]
    own_rows = hidden.shape[0]
    for layer_index in range(LAYERS):
        key_slab = hist_keys[layer_index, 0]
        value_slab = hist_values[layer_index, 0]
        queries = jax.nn.silu(
            jnp.dot(hidden, w_query[layer_index], preferred_element_type=jnp.float32)
        ).astype(jnp.bfloat16)
        gating = jax.nn.silu(
            jnp.dot(hidden, w_gate[layer_index], preferred_element_type=jnp.float32)
        )
        all_queries = lax.all_gather(queries, "hist", axis=0, tiled=True)

        def by_block(
            begin_row, row_count, all_queries=all_queries, key_slab=key_slab, value_slab=value_slab
        ):
            return attend_rows(all_queries, key_slab, value_slab, limits)

        summed = lax.psum_scatter(
            by_block(jnp.int32(0), own_rows * lax.axis_size("hist")),
            "hist",
            scatter_dimension=0,
            tiled=True,
        )
        hidden = finish(hidden, summed, gating, w_out[layer_index], ln_gain[layer_index])
    return hidden[None]


def solution(mesh):
    return jax.shard_map(
        per_device,
        mesh=mesh,
        in_specs=(
            P(("groups", "users"), "hist", None),
            P(None, ("groups", "users"), "hist", None),
            P(None, ("groups", "users"), "hist", None),
            P(("groups", "users")),
            P(("groups", "users"), None),
            P(),
            P(),
            P(),
            P(),
        ),
        out_specs=P(("groups", "users"), "hist", None),
        check_vma=False,
    )
```

profile of v0, /device:TPU:0, one launch (start us, length us, event | category | flops | bytes accessed | tf_op | source)
XLA Modules:
  0.0 282.8 jit_solution(4211287939097694233)
XLA Ops:
  6.5 0.0 all-gather.3.cloned.1.call-start
  6.5 2.8 %multiply_convert_fusion.3 = bf16[64,1024]{1,0:T(8,128)(2,1)} fusion(bf16[2,1024,1024]{2,1,0:T(8,128)(2,1)} %param.14, bf16[1,64,1024]{2,1,0:T(8,128)(2,1)} %param.9), kind=kOutput, calls=%fused_computation.41 | convolution fusion | flops 134545408 | bytes 2359296 | tf_op jit(solution)/shard_map/dot_general | solution.py:52
  9.4 0.0 all-gather.3.cloned.1.call-update
  9.4 0.0 reduce-scatter.3.cloned.1.call-start
  9.5 5.2 %fusion.80 = (bf16[1,1,1536,1024]{3,2,1,0:T(8,128)(2,1)S(1)}, bf16[1,1,1536,1024]{3,2,1,0:T(8,128)(2,1)}) fusion(bf16[2,1,1536,1024]{3,2,1,0:T(8,128)(2,1)} %param.10), kind=kLoop, calls=%fused_computation.67 | loop fusion | bytes 12582912 | tf_op jit(solution)/shard_map/slice | solution.py:49
  14.7 4.7 %copy.30 = bf16[1,1,1536,1024]{2,3,1,0:T(8,128)(2,1)} copy(bf16[1,1,1536,1024]{3,2,1,0:T(8,128)(2,1)} %get-tuple-element.6) | data formatting | bytes 6291456
  19.3 6.2 %fusion.81 = (bf16[1,1,1536,1024]{3,2,1,0:T(8,128)(2,1)}, bf16[1,1,1536,1024]{3,2,1,0:T(8,128)(2,1)}) fusion(bf16[2,1,1536,1024]{3,2,1,0:T(8,128)(2,1)} %param.11), kind=kLoop, calls=%fused_computation.68 | loop fusion | bytes 12582912 | tf_op jit(solution)/shard_map/slice | solution.py:50
  25.6 0.0 copy-start.2
  25.6 4.7 %copy.19 = bf16[1,1,1536,1024]{2,3,1,0:T(8,128)(2,1)} copy(bf16[1,1,1536,1024]{3,2,1,0:T(8,128)(2,1)} %get-tuple-element.8) | data formatting | bytes 6291456 | tf_op jit(solution)/shard_map/slice | solution.py:50
  30.9 0.0 copy-done.2
  31.0 1.4 iota_compare_fusion
  32.4 20.2 %all-gather.3.cloned.1.call-done = bf16[512,1024]{1,0:T(8,128)(2,1)} async-done(((bf16[64,1024]{1,0:T(8,128)(2,1)}), bf16[512,1024]{1,0:T(8,128)(2,1)}) %all-gather.3.cloned.1.call-update) | async-done | bytes 1048592 | tf_op jit(solution)/shard_map/all_gather | solution.py:57
  52.6 15.0 %fusion = f32[8,512,128]{1,2,0:T(8,128)} fusion(bf16[1536,8,128]{0,2,1:T(8,128)(2,1)} %bitcast.88, bf16[1536,8,128]{0,2,1:T(8,128)(2,1)} %bitcast.87, pred[512,1536]{1,0:T(8,128)(4,1)} %iota_compare_fusion, bf16[512,1024]{1,0:T(8,128)(2,1)} %all-gather.3.cloned.1.call-done), kind=kOutput, calls=%fused_computation.3 | convolution fusion | flops 3265265664 | bytes 10223616 | tf_op jit(solution)/shard_map/hrj,jhd->rhd/dot_general | solution.py:28
  67.6 0.0 copy-start.1
  67.6 0.0 copy-start.3
  67.6 3.0 %copy.28 = f32[512,1024]{1,0:T(8,128)} copy(f32[512,1024]{0,1:T(8,128)} %bitcast.92) | data formatting | bytes 4194304 | tf_op jit(solution)/shard_map/reshape | solution.py:29
  70.6 0.0 reduce-scatter.3.cloned.1.call-update
  70.6 0.0 all-gather.5.cloned.1.call-start
  70.7 0.0 copy-done.1
  70.7 67.1 %reduce-scatter.3.cloned.1.call-done = f32[64,1024]{1,0:T(8,128)} async-done(((f32[512,1024]{1,0:T(8,128)}), f32[64,1024]{1,0:T(8,128)}) %reduce-scatter.3.cloned.1.call-update) | async-done | bytes 262160 | tf_op jit(solution)/shard_map/reduce_scatter | solution.py:64
  137.7 1.1 reduce_sum.36
  138.8 1.1 multiply_reduce_fusion.1
  140.0 0.0 copy-done.3
  140.0 3.2 %fusion.29 = bf16[64,1024]{1,0:T(8,128)(2,1)S(1)} fusion(bf16[2,1024,1024]{2,1,0:T(8,128)(2,1)} %param.16, bf16[2,1024,1024]{2,1,0:T(8,128)(2,1)} %param.15, f32[64,1024]{1,0:T(8,128)} %reduce-scatter.3.cloned.1.call-done, bf16[1,64,1024]{2,1,0:T(8,128)(2,1)S(1)} %copy-done.3, f32[1024]{0:T(1024)S(1)} %bitcast.95, f32[64]{0:T(128)S(1)} %add_rsqrt_fusion.1, ...), kind=kOutput, calls=%fused_computation.26 | convolution fusion | flops 269221888 | bytes 4854784 | tf_op jit(solution)/shard_map/dot_general | solution.py:38
  143.2 2.8 multiply_convert_fusion.1
  146.0 0.0 all-gather.5.cloned.1.call-update
  146.0 0.2 reduce-scatter.5.cloned.1.call-start
  146.2 3.0 %copy.31 = bf16[1,1,1536,1024]{2,3,1,0:T(8,128)(2,1)} copy(bf16[1,1,1536,1024]{3,2,1,0:T(8,128)(2,1)S(1)} %get-tuple-element.5) | data formatting | bytes 6291456
  149.2 0.0 copy-start
  149.3 4.8 %copy.24 = bf16[1,1,1536,1024]{2,3,1,0:T(8,128)(2,1)} copy(bf16[1,1,1536,1024]{3,2,1,0:T(8,128)(2,1)} %get-tuple-element.7) | data formatting | bytes 6291456 | tf_op jit(solution)/shard_map/slice | solution.py:50
  154.1 31.4 %all-gather.5.cloned.1.call-done = bf16[512,1024]{1,0:T(8,128)(2,1)} async-done(((bf16[64,1024]{1,0:T(8,128)(2,1)}), bf16[512,1024]{1,0:T(8,128)(2,1)}) %all-gather.5.cloned.1.call-update) | async-done | bytes 1048592 | tf_op jit(solution)/shard_map/all_gather | solution.py:57
  185.5 0.0 copy-done
  185.5 14.6 %fusion.1 = f32[8,512,128]{1,2,0:T(8,128)} fusion(bf16[1536,8,128]{0,2,1:T(8,128)(2,1)} %bitcast.90, bf16[1536,8,128]{0,2,1:T(8,128)(2,1)S(1)} %bitcast.89, pred[512,1536]{1,0:T(8,128)(4,1)} %iota_compare_fusion, bf16[512,1024]{1,0:T(8,128)(2,1)} %all-gather.5.cloned.1.call-done), kind=kOutput, calls=%fused_computation.4 | convolution fusion | flops 3265265664 | bytes 10223616 | tf_op jit(solution)/shard_map/hrj,jhd->rhd/dot_general | solution.py:28
  200.1 2.9 %copy.29 = f32[512,1024]{1,0:T(8,128)} copy(f32[512,1024]{0,1:T(8,128)} %bitcast.91) | data formatting | bytes 4194304 | tf_op jit(solution)/shard_map/reshape | solution.py:29
  203.0 0.0 reduce-scatter.5.cloned.1.call-update
  203.0 67.1 %reduce-scatter.5.cloned.1.call-done = f32[64,1024]{1,0:T(8,128)} async-done(((f32[512,1024]{1,0:T(8,128)}), f32[64,1024]{1,0:T(8,128)}) %reduce-scatter.5.cloned.1.call-update) | async-done | bytes 262160 | tf_op jit(solution)/shard_map/reduce_scatter | solution.py:64
  270.1 1.1 reduce_sum.38
  271.2 1.1 multiply_reduce_fusion
  272.4 3.9 %fusion.32 = bf16[1,64,1024]{2,1,0:T(8,128)(2,1)} fusion(bf16[2,1024,1024]{2,1,0:T(8,128)(2,1)} %param.16, bf16[64,1024]{1,0:T(8,128)(2,1)S(1)} %fusion.29, bf16[2,1024,1024]{2,1,0:T(8,128)(2,1)} %param.15, f32[64,1024]{1,0:T(8,128)} %reduce-scatter.5.cloned.1.call-done, f32[1024]{0:T(1024)S(1)} %bitcast.94, f32[64]{0:T(128)S(1)} %add_rsqrt_fusion, ...), kind=kOutput, calls=%fused_computation.27 | convolution fusion | flops 269221888 | bytes 4854784 | tf_op jit(solution)/shard_map/dot_general | solution.py:38
  (6 shorter events, 0.0 us)
Async XLA Ops:
  6.5 46.0 %all-gather.3.cloned.1.call-start = ((), (), s32[]{:S(2)}) async-start(), calls=%async_computation.2 | async-start | bytes 1179648 | tf_op jit(solution)/shard_map/all_gather | solution.py:57
  9.4 128.3 %reduce-scatter.3.cloned.1.call-start = ((), (), s32[]{:S(2)}) async-start(), calls=%async_computation.3 | async-start | bytes 2359296 | tf_op jit(solution)/shard_map/reduce_scatter | solution.py:64
  25.6 5.4 %copy-start.2 = (s32[1,512]{1,0:T(1,128)S(1)}, s32[1,512]{1,0:T(1,128)}, u32[]{:S(2)}) copy-start(s32[1,512]{1,0:T(1,128)} %param.13) | copy-start | bytes 6148
  67.6 3.1 %copy-start.1 = (f32[2,1024]{1,0:T(2,128)S(1)}, f32[2,1024]{1,0:T(2,128)}, u32[]{:S(2)}) copy-start(f32[2,1024]{1,0:T(2,128)} %param.17) | copy-start | bytes 24580
  67.6 72.4 %copy-start.3 = (bf16[1,64,1024]{2,1,0:T(8,128)(2,1)S(1)}, bf16[1,64,1024]{2,1,0:T(8,128)(2,1)}, u32[]{:S(2)}) copy-start(bf16[1,64,1024]{2,1,0:T(8,128)(2,1)} %param.9) | copy-start | bytes 393220
  70.6 114.9 %all-gather.5.cloned.1.call-start = ((), (), s32[]{:S(2)}) async-start(), calls=%async_computation.4 | async-start | bytes 1179648 | tf_op jit(solution)/shard_map/all_gather | solution.py:57
  146.0 124.1 %reduce-scatter.5.cloned.1.call-start = ((), (), s32[]{:S(2)}) async-start(), calls=%async_computation.5 | async-start | bytes 2359296 | tf_op jit(solution)/shard_map/reduce_scatter | solution.py:64
  149.2 36.3 %copy-start = (bf16[1,1,1536,1024]{2,3,1,0:T(8,128)(2,1)S(1)}, bf16[1,1,1536,1024]{2,3,1,0:T(8,128)(2,1)}, u32[]{:S(2)}) copy-start(bf16[1,1,1536,1024]{2,3,1,0:T(8,128)(2,1)} %copy.31) | copy-start | bytes 9437188
Sparse Core Ops, SparseCore 0:
  9.5 42.9 all-gather.2
  70.7 66.9 reduce-scatter.2
  146.1 39.3 all-gather.4
  203.2 66.9 reduce-scatter.4
where the time goes:
time: 283 us
  waiting for transfers between devices  186 us (66%)
  matrix products  42.3 us (15%)
  local copies, waits for them, and re-layouts  34.6 us (12%)
  between operations  13.9 us (5%)
  other arithmetic  5.86 us (2%)
    reduce_scatter x2, waiting for transfers between devices, per_device(): lax.psum_scatter(by_block(jnp.int32(0), own_rows * lax.axis_size('hist'))...  134 us
    all_gather x2, waiting for transfers between devices, per_device(): all_queries = lax.all_gather(queries, 'hist', axis=0, tiled=True)  51.6 us
    dot_general x2, matrix products, attend_rows(): jnp.einsum('hrj,jhd->rhd', weights, value_heads, preferred_element_type=j...  29.6 us
    slice x3, local copies, waits for them, and re-layouts, per_device(): value_slab = hist_values[layer_index, 0]  15.8 us
    unnamed x10, local copies, waits for them, and re-layouts  7.69 us
    dot_general x2, matrix products, finish(): update = jnp.dot(normed, out_weight, preferred_element_type=jnp.float32)  7.08 us
    reshape x2, local copies, waits for them, and re-layouts, attend_rows(): return output.reshape(row_count, D)  5.88 us
  transfers between devices with their start and end apart: 4, of which 4 were waited for; matrix products, arithmetic and copies ran while one was open for 11% of the time, Pallas kernels for 0%

commit v1 on v0

v1 whole, which is shorter than its diff:
```python
import functools
import math

import jax
import jax.numpy as jnp
from jax import lax
from jax.experimental import pallas as pl
from jax.experimental.pallas import tpu as pltpu
from jax.sharding import PartitionSpec as P

HEADS = 8
MESH = pl.DeviceIdType.MESH


def half_silu(t):
    return t + t * jnp.tanh(t)


def tile_of(size, most):
    while size % most:
        most //= 2
    return most


def kernel(
    ny, nz, lim_ref, tgt_ref, keys_ref, vals_ref, wq_ref, wg_ref, wo_ref, gain_ref, out_ref,
    kbuf, vbuf, wqb, wgb, wob, q_all, pair, s1, r1, s2, r2, gate, hid, proj, normed,
    in_sem, zs_sem, zr_sem, fs_sem, fr_sem, s1_sem, r1_sem, s2_sem, r2_sem,
):
    me = lax.axis_index("hist")
    z, y = me // ny, me % ny
    layers, hist, width = kbuf.shape
    rows = tgt_ref.shape[0]
    head = width // HEADS
    factor = 0.5 / math.sqrt(head)
    wide = tile_of(width, 256)
    chunk = tile_of(hist, 256)

    def at(zz, yy):
        return {"hist": zz * ny + yy}

    loads = []
    for l in range(layers):
        for k, (src, dst) in enumerate(
            ((wq_ref, wqb), (keys_ref, kbuf), (vals_ref, vbuf), (wg_ref, wgb), (wo_ref, wob))
        ):
            copy = pltpu.make_async_copy(src.at[l], dst.at[l], in_sem.at[l, k])
            copy.start()
            loads.append(copy)

    barrier = pltpu.get_barrier_semaphore()
    for j in range(1, nz):
        pl.semaphore_signal(barrier, inc=1, device_id=at((z + j) % nz, y), device_id_type=MESH)
    if ny == 2:
        pl.semaphore_signal(barrier, inc=1, device_id=at(z, 1 - y), device_id_type=MESH)
    hid[...] = tgt_ref[...]

    def project(w_ref, store):
        def body(i, carry):
            cols = pl.ds(pl.multiple_of(i * wide, wide), wide)
            v = jnp.dot(hid[...], w_ref[:, cols], preferred_element_type=jnp.float32)
            store(cols, half_silu(v * 0.5))
            return carry

        lax.fori_loop(0, width // wide, body, 0)

    sends = []

    def send(src, dst, ss, rs, dev):
        copy = pltpu.make_async_remote_copy(
            src_ref=src, dst_ref=dst, send_sem=ss, recv_sem=rs, device_id=dev, device_id_type=MESH
        )
        copy.start()
        sends.append(copy)
        return copy

    for l in range(layers):
        base = l * 5
        loads[base].wait()

        def put_q(cols, v):
            q_all[l, z, y, :, cols] = v.astype(jnp.bfloat16)

        project(wqb.at[l], put_q)
        if l == 0:
            pl.semaphore_wait(barrier, nz - 1 + ny - 1)

        mine = q_all.at[l, z, y]
        fy = [None] * nz
        zc = [None] * nz
        if ny == 2:
            fy[0] = send(mine, mine, fs_sem.at[l, 0], fr_sem.at[l, 0], at(z, 1 - y))
        for j in range(1, nz):
            zc[j] = send(mine, mine, zs_sem.at[l, j], zr_sem.at[l, j], at((z + j) % nz, y))

        loads[base + 3].wait()

        def put_gate(cols, v):
            gate[:, cols] = v

        project(wgb.at[l], put_gate)
        loads[base + 1].wait()
        loads[base + 2].wait()
        c1 = [None] * nz
        c2 = [None] * nz

        def attend(j):
            zj = (z - j + nz) % nz
            limit = lim_ref[pl.ds(pl.multiple_of(zj * ny * rows, ny * rows), ny * rows), :]

            def body(h, carry):
                cols = pl.ds(pl.multiple_of(h * head, head), head)
                q = q_all[l, zj, :, :, cols].reshape(ny * rows, head)
                total = jnp.zeros((ny * rows, head), jnp.float32)
                for c in range(0, hist, chunk):
                    s = lax.dot_general(
                        q, kbuf[l, c : c + chunk, cols], (((1,), (1,)), ((), ())),
                        preferred_element_type=jnp.float32,
                    )
                    w = half_silu(s * factor)
                    pos = lax.broadcasted_iota(jnp.int32, s.shape, 1) + c
                    w = jnp.where(pos < limit, w, 0.0).astype(jnp.bfloat16)
                    total += jnp.dot(
                        w, vbuf[l, c : c + chunk, cols], preferred_element_type=jnp.float32
                    )
                pair[j, :, :, cols] = total.reshape(ny, rows, head)
                return carry

            lax.fori_loop(0, HEADS, body, 0)

        def reduce(j):
            if j == 0:
                return
            term = pair[j, y]
            if ny == 2:
                c1[j].wait_recv()
                term = term + r1[l, j].astype(jnp.float32)
            s2[l, j] = term.astype(jnp.bfloat16)
            c2[j] = send(
                s2.at[l, j], r2.at[l, j], s2_sem.at[l, j], r2_sem.at[l, j],
                at((z - j + nz) % nz, y),
            )

        for j in range(nz):
            if j + 1 < nz:
                zc[j + 1].wait_recv()
                if ny == 2:
                    block = q_all.at[l, (z - j - 1 + nz) % nz, y]
                    fy[j + 1] = send(
                        block, block, fs_sem.at[l, j + 1], fr_sem.at[l, j + 1], at(z, 1 - y)
                    )
            if ny == 2:
                fy[j].wait_recv()
            attend(j)
            if ny == 2:
                s1[l, j] = pair[j, 1 - y].astype(jnp.bfloat16)
                c1[j] = send(
                    s1.at[l, j], r1.at[l, j], s1_sem.at[l, j], r1_sem.at[l, j], at(z, 1 - y)
                )
            if j > 0:
                reduce(j - 1)
        reduce(nz - 1)

        summed = pair[0, y]
        if ny == 2:
            c1[0].wait_recv()
            summed = summed + r1[l, 0].astype(jnp.float32)
        for j in range(1, nz):
            c2[j].wait_recv()
            summed = summed + r2[l, j].astype(jnp.float32)
        centre = jnp.mean(summed, axis=-1, keepdims=True)
        summed = summed - centre
        spread = jnp.mean(jnp.square(summed), axis=-1, keepdims=True)
        normed[...] = (
            summed * lax.rsqrt(spread + 1e-05) * gain_ref[l : l + 1, :] * gate[...]
        ).astype(jnp.bfloat16)
        loads[base + 4].wait()
        target = out_ref if l == layers - 1 else proj

        def out_body(i, carry):
            cols = pl.ds(pl.multiple_of(i * wide, wide), wide)
            update = jnp.dot(normed[...], wob[l, :, cols], preferred_element_type=jnp.float32)
            target[:, cols] = (hid[:, cols].astype(jnp.float32) + update).astype(jnp.bfloat16)
            return carry

        lax.fori_loop(0, width // wide, out_body, 0)
        if l < layers - 1:
            hid[...] = proj[...]

    for copy in sends:
        copy.wait_send()


def inner_size(mesh):
    try:
        spot = mesh.axis_names.index("hist")
        line = mesh.devices.transpose(
            [spot] + [a for a in range(mesh.devices.ndim) if a != spot]
        ).reshape(mesh.devices.shape[spot], -1)[:, 0]
        ys = len({d.coords[1] for d in line})
    except (AttributeError, ValueError):
        ys = 1
    return ys if ys in (1, 2) and len(line) % ys == 0 else 1


def per_device(
    ny, targets, hist_keys, hist_values, lengths, cuts, w_query, w_gate, w_out, ln_gain
):
    layers, _, hist, width = hist_keys.shape
    rows = targets.shape[1]
    n = lax.axis_size("hist")
    nz = n // ny
    offset = lax.axis_index("hist") * hist
    limits = (jnp.minimum(cuts[0], lengths[0]) - offset)[:, None]
    bf, f32 = jnp.bfloat16, jnp.float32
    vmem = pl.BlockSpec(memory_space=pltpu.VMEM)
    hbm = pl.BlockSpec(memory_space=pl.ANY)
    dma = pltpu.SemaphoreType.DMA
    refined = pl.pallas_call(
        functools.partial(kernel, ny, nz),
        out_shape=jax.ShapeDtypeStruct((rows, width), bf),
        in_specs=[vmem, vmem, hbm, hbm, hbm, hbm, hbm, vmem],
        out_specs=vmem,
        scratch_shapes=[
            pltpu.VMEM((layers, hist, width), bf),
            pltpu.VMEM((layers, hist, width), bf),
            pltpu.VMEM((layers, width, width), bf),
            pltpu.VMEM((layers, width, width), bf),
            pltpu.VMEM((layers, width, width), bf),
            pltpu.VMEM((layers, nz, ny, rows, width), bf),
            pltpu.VMEM((nz, ny, rows, width), f32),
            pltpu.VMEM((layers, nz, rows, width), bf),
            pltpu.VMEM((layers, nz, rows, width), bf),
            pltpu.VMEM((layers, nz, rows, width), bf),
            pltpu.VMEM((layers, nz, rows, width), bf),
            pltpu.VMEM((rows, width), f32),
            pltpu.VMEM((rows, width), bf),
            pltpu.VMEM((rows, width), bf),
            pltpu.VMEM((rows, width), bf),
            dma((layers, 5)),
        ]
        + [dma((layers, nz))] * 8,
        compiler_params=pltpu.CompilerParams(
            collective_id=0, has_side_effects=True, vmem_limit_bytes=60 * 2**20
        ),
    )(
        limits, targets[0], hist_keys[:, 0], hist_values[:, 0], w_query, w_gate, w_out, ln_gain
    )
    return refined[None]


def solution(mesh):
    return jax.shard_map(
        functools.partial(per_device, inner_size(mesh)),
        mesh=mesh,
        in_specs=(
            P(("groups", "users"), "hist", None),
            P(None, ("groups", "users"), "hist", None),
            P(None, ("groups", "users"), "hist", None),
            P(("groups", "users")),
            P(("groups", "users"), None),
            P(),
            P(),
            P(),
            P(),
        ),
        out_specs=P(("groups", "users"), "hist", None),
        check_vma=False,
    )
```

time: 283 us -> 91.1 us (0.32)
  waiting for transfers between devices: 186 us -> 0 us
  Pallas kernels: 0 us -> 86.8 us
  matrix products: 42.3 us -> 0 us
  local copies, waits for them, and re-layouts: 34.6 us -> 2.42 us
  between operations: 13.9 us -> 0.66 us
  other arithmetic: 5.86 us -> 0.69 us
    reduce_scatter x2 -> x0, waiting for transfers between devices: 134 us -> none  [per_device(): lax.psum_scatter(by_block(jnp.int32(0), own_rows * lax.axis_size('hist'))...]
    pallas_call x0 -> x1, Pallas kernels: none -> 86.8 us  [per_device(): pl.pallas_call(functools.partial(kernel, ny, nz), out_shape=jax.ShapeDtyp...]
    all_gather x2 -> x0, waiting for transfers between devices: 51.6 us -> none  [per_device(): all_queries = lax.all_gather(queries, 'hist', axis=0, tiled=True)]
    dot_general x6 -> x0, matrix products: 42.3 us -> none  [the longest x2 29.6 us: attend_rows(): jnp.einsum('hrj,jhd->rhd', weights, value_heads, preferred_element_type=j...]
    slice x5 -> x0, local copies, waits for them, and re-layouts: 21 us -> none  [the longest x3 15.8 us: per_device(): value_slab = hist_values[layer_index, 0]]
    unnamed x10 -> x1, local copies, waits for them, and re-layouts: 7.69 us -> 1.57 us
    reshape x2 -> x0, local copies, waits for them, and re-layouts: 5.88 us -> none  [attend_rows(): return output.reshape(row_count, D)]
    reduce_sum x4 -> x0, other arithmetic: 4.43 us -> none  [the longest x2 2.3 us: finish(): spread = jnp.mean(jnp.square(summed - centre), axis=-1, keepdims=True)]
  transfers between devices with their start and end apart: 4 -> 0, of which waited for: 4 -> 0; matrix products, arithmetic and copies ran while one was open for 11% -> 0% of each run, Pallas kernels for 0% -> 0%
where the time goes in v1:
time: 91.1 us; the launch traced here: 90.6 us
  Pallas kernels  86.8 us (95%)
  local copies, waits for them, and re-layouts  2.42 us (3%)
    pallas_call x1, Pallas kernels, per_device(): pl.pallas_call(functools.partial(kernel, ny, nz), out_shape=jax.ShapeDtyp...  86.8 us

profile of v1, /device:TPU:0, one launch (start us, length us, event | category | flops | bytes accessed | tf_op | source)
XLA Modules:
  0.0 90.6 jit_solution(18005248507420189199)
XLA Ops:
  0.7 0.7 subtract_bitcast_fusion
  1.3 0.9 copy.10.lim_ref
  2.2 86.8 %shard_map.91 = bf16[64,1024]{1,0:T(8,128)(2,1)} custom-call(s32[512,1]{1,0:T(8,128)} %copy.10.lim_ref, bf16[64,1024]{1,0:T(8,128)(2,1)} %bitcast.11, bf16[2,1536,1024]{2,1,0:T(8,128)(2,1)} %bitcast.8, bf16[2,1536,1024]{2,1,0:T(8,128)(2,1)} %bitcast.9, bf16[2,1024,1024]{2,1,0:T(8,128)(2,1)} %wq_ref.1, bf16[2,1024,1024]{2,1,0:T(8,128)(2,1)} %wg_ref.1, ...), custom_call_target="tpu_custom_call" | custom-call | tf_op jit(solution)/shard_map/pallas_call | solution.py:219
  89.0 1.6 %copy.13 = bf16[1,64,1024]{2,1,0:T(8,128)(2,1)} copy(bf16[1,64,1024]{2,1,0:T(8,128)(2,1)} %bitcast.10) | data formatting | bytes 262144

commit v2 on v1

v2 whole, which is shorter than its diff:
```python
import functools
import math

import jax
import jax.numpy as jnp
from jax import lax
from jax.experimental import pallas as pl
from jax.experimental.pallas import tpu as pltpu
from jax.sharding import PartitionSpec as P

HEADS = 8
GROUPS = 2
PARTS = 2
CHUNK = 256
UNROLL = 2
MESH = pl.DeviceIdType.MESH


def half_silu(t):
    return t + t * jnp.tanh(t)


def tile_of(size, most):
    while size % most:
        most //= 2
    return most


def kernel(
    ny, nz, lim_ref, tgt_ref, keys_ref, vals_ref, wq_ref, wg_ref, wo_ref, gain_ref, out_ref,
    kbuf, vbuf, wqb, wgb, wob, q_all, res, s1, r1, s2, r2, gate, hid, normed,
    in_sem, zs_sem, zr_sem, fs_sem, fr_sem, s1_sem, r1_sem, s2_sem, r2_sem,
):
    me = lax.axis_index("hist")
    z, y = me // ny, me % ny
    layers, hist, width = kbuf.shape
    parts = s1.shape[2]
    rows = tgt_ref.shape[0] // GROUPS
    head = width // HEADS
    factor = 0.5 / math.sqrt(head)
    wide = tile_of(width, 256)
    chunk = tile_of(hist, CHUNK)
    span = width // parts
    total_rows = nz * ny * rows
    bf, f32 = jnp.bfloat16, jnp.float32

    def at(zz, yy):
        return {"hist": zz * ny + yy}

    loads = []
    for l in range(layers):
        for k, (src, dst) in enumerate(
            ((wq_ref, wqb), (keys_ref, kbuf), (vals_ref, vbuf), (wg_ref, wgb), (wo_ref, wob))
        ):
            copy = pltpu.make_async_copy(src.at[l], dst.at[l], in_sem.at[l, k])
            copy.start()
            loads.append(copy)

    barrier = pltpu.get_barrier_semaphore()
    for j in range(1, nz):
        pl.semaphore_signal(barrier, inc=1, device_id=at((z + j) % nz, y), device_id_type=MESH)
    if ny == 2:
        pl.semaphore_signal(barrier, inc=1, device_id=at(z, 1 - y), device_id_type=MESH)
    hid[...] = tgt_ref[...].reshape(hid.shape)

    copies = {}

    def send(name, src, dst, ss, rs, dev):
        copy = pltpu.make_async_remote_copy(
            src_ref=src, dst_ref=dst, send_sem=ss, recv_sem=rs, device_id=dev, device_id_type=MESH
        )
        copy.start()
        copies[name] = copy

    def columns(i, size):
        return pl.ds(pl.multiple_of(i * size, size), size)

    def project(w_ref, g0, g1, store):
        def body(i, carry):
            cols = columns(i, wide)
            x = hid[g0:g1].reshape((g1 - g0) * rows, width)
            v = jnp.dot(x, w_ref[:, cols], preferred_element_type=f32)
            v = half_silu(v * 0.5)
            for g in range(g0, g1):
                store(g, cols, v[(g - g0) * rows : (g - g0 + 1) * rows])
            return carry

        lax.fori_loop(0, width // wide, body, 0, unroll=2)

    def query(l, g0, g1):
        def store(g, cols, v):
            q_all[l, g, z, y, :, cols] = v.astype(bf)

        project(wqb.at[l], g0, g1, store)

    def spread(l, g):
        mine = q_all.at[l, g, z, y]
        if ny == 2:
            send(("f", l, g, 0), mine, mine, fs_sem.at[l, g, 0], fr_sem.at[l, g, 0], at(z, 1 - y))
        for j in range(1, nz):
            send(
                ("z", l, g, j), mine, mine, zs_sem.at[l, g, j], zr_sem.at[l, g, j],
                at((z + j) % nz, y),
            )

    def gating(l, g0, g1):
        def store(g, cols, v):
            gate[g, :, cols] = v

        project(wgb.at[l], g0, g1, store)

    def forward(l, g):
        for j in range(1, nz):
            copies["z", l, g, j].wait_recv()
            if ny == 2:
                block = q_all.at[l, g, (z - j + nz) % nz, y]
                send(
                    ("f", l, g, j), block, block, fs_sem.at[l, g, j], fr_sem.at[l, g, j],
                    at(z, 1 - y),
                )

    def arrive(l, g):
        if ny == 2:
            for j in range(nz):
                copies["f", l, g, j].wait_recv()

    def attend(l, g, p):
        def body(i, carry):
            cols = columns(p * (HEADS // parts) + i, head)
            q = q_all[l, g, :, :, :, cols].reshape(total_rows, head)
            limit = lim_ref[g]
            total = jnp.zeros((total_rows, head), f32)
            for c in range(0, hist, chunk):
                s = lax.dot_general(
                    q, kbuf[l, c : c + chunk, cols], (((1,), (1,)), ((), ())),
                    preferred_element_type=f32,
                )
                w = half_silu((s * factor).astype(bf))
                pos = lax.broadcasted_iota(jnp.int32, s.shape, 1) + c
                w = jnp.where(pos < limit, w, jnp.bfloat16(0.0))
                total += jnp.dot(w, vbuf[l, c : c + chunk, cols], preferred_element_type=f32)
            res[g, :, :, :, cols] = total.reshape(nz, ny, rows, head)
            return carry

        lax.fori_loop(0, HEADS // parts, body, 0, unroll=UNROLL)
        if ny == 2:
            s1[l, g, p] = res[g, :, 1 - y, :, p * span : (p + 1) * span].astype(bf)
            send(
                ("1", l, g, p), s1.at[l, g, p], r1.at[l, g, p], s1_sem.at[l, g, p],
                r1_sem.at[l, g, p], at(z, 1 - y),
            )

    def reduce(l, g, p):
        if ny == 2:
            copies["1", l, g, p].wait_recv()
        for j in range(1, nz):
            zj = (z - j + nz) % nz
            term = res[g, zj, y, :, p * span : (p + 1) * span]
            if ny == 2:
                term = term + r1[l, g, p, zj].astype(f32)
            s2[l, g, p, j] = term.astype(bf)
            send(
                ("2", l, g, p, j), s2.at[l, g, p, j], r2.at[l, g, p, j], s2_sem.at[l, g, p, j],
                r2_sem.at[l, g, p, j], at(zj, y),
            )

    def finish(l, g):
        sums = []
        for p in range(parts):
            term = res[g, z, y, :, p * span : (p + 1) * span]
            if ny == 2:
                term = term + r1[l, g, p, z].astype(f32)
            for j in range(1, nz):
                copies["2", l, g, p, j].wait_recv()
                term = term + r2[l, g, p, j].astype(f32)
            sums.append(term)
        centre = sum(jnp.sum(t, axis=-1, keepdims=True) for t in sums) / width
        sums = [t - centre for t in sums]
        variance = sum(jnp.sum(jnp.square(t), axis=-1, keepdims=True) for t in sums) / width
        scale = lax.rsqrt(variance + 1e-05)
        for p, t in enumerate(sums):
            cols = slice(p * span, (p + 1) * span)
            normed[g, :, cols] = (t * scale * gain_ref[l : l + 1, cols] * gate[g, :, cols]).astype(bf)

        def body(i, carry):
            cols = columns(i, wide)
            update = jnp.dot(normed[g], wob[l, :, cols], preferred_element_type=f32)
            new = (hid[g, :, cols].astype(f32) + update).astype(bf)
            if l == layers - 1:
                out_ref[g * rows : (g + 1) * rows, cols] = new
            else:
                hid[g, :, cols] = new
            return carry

        lax.fori_loop(0, width // wide, body, 0, unroll=2)

    for l in range(layers):
        wait = loads[l * 5 : l * 5 + 5]
        if l == 0:
            wait[0].wait()
            query(0, 0, GROUPS)
            pl.semaphore_wait(barrier, nz - 1 + ny - 1)
            for g in range(GROUPS):
                spread(0, g)
            wait[3].wait()
            gating(0, 0, GROUPS)
        else:
            prev = GROUPS - 1
            wait[0].wait()
            for g in range(GROUPS):
                if g == prev:
                    reduce(l - 1, prev, parts - 1)
                finish(l - 1, g)
                query(l, g, g + 1)
                spread(l, g)
            wait[3].wait()
            gating(l, 0, GROUPS)
        wait[1].wait()
        wait[2].wait()
        wait[4].wait()
        forward(l, 0)
        arrive(l, 0)
        for g in range(GROUPS):
            for p in range(parts):
                attend(l, g, p)
                if p == 0 and g + 1 < GROUPS:
                    forward(l, g + 1)
                if p > 0:
                    reduce(l, g, p - 1)
                elif g > 0:
                    reduce(l, g - 1, parts - 1)
            if g + 1 < GROUPS:
                arrive(l, g + 1)
    last = layers - 1
    for g in range(GROUPS):
        if g == GROUPS - 1:
            reduce(last, g, parts - 1)
        finish(last, g)

    for copy in copies.values():
        copy.wait_send()


def inner_size(mesh):
    try:
        spot = mesh.axis_names.index("hist")
        line = mesh.devices.transpose(
            [spot] + [a for a in range(mesh.devices.ndim) if a != spot]
        ).reshape(mesh.devices.shape[spot], -1)[:, 0]
        ys = len({d.coords[1] for d in line})
    except (AttributeError, ValueError):
        ys = 1
    return ys if ys in (1, 2) and len(line) % ys == 0 else 1


def per_device(
    ny, targets, hist_keys, hist_values, lengths, cuts, w_query, w_gate, w_out, ln_gain
):
    layers, _, hist, width = hist_keys.shape
    rows = targets.shape[1]
    n = lax.axis_size("hist")
    nz = n // ny
    offset = lax.axis_index("hist") * hist
    rows //= GROUPS
    limits = jnp.minimum(cuts[0], lengths[0]) - offset
    limits = limits.reshape(n, GROUPS, rows).transpose(1, 0, 2).reshape(GROUPS, n * rows, 1)
    bf, f32 = jnp.bfloat16, jnp.float32
    vmem = pl.BlockSpec(memory_space=pltpu.VMEM)
    hbm = pl.BlockSpec(memory_space=pl.ANY)
    dma = pltpu.SemaphoreType.DMA
    span = width // PARTS
    refined = pl.pallas_call(
        functools.partial(kernel, ny, nz),
        out_shape=jax.ShapeDtypeStruct((GROUPS * rows, width), bf),
        in_specs=[vmem, vmem, hbm, hbm, hbm, hbm, hbm, vmem],
        out_specs=vmem,
        scratch_shapes=[
            pltpu.VMEM((layers, hist, width), bf),
            pltpu.VMEM((layers, hist, width), bf),
            pltpu.VMEM((layers, width, width), bf),
            pltpu.VMEM((layers, width, width), bf),
            pltpu.VMEM((layers, width, width), bf),
            pltpu.VMEM((layers, GROUPS, nz, ny, rows, width), bf),
            pltpu.VMEM((GROUPS, nz, ny, rows, width), f32),
            pltpu.VMEM((layers, GROUPS, PARTS, nz, rows, span), bf),
            pltpu.VMEM((layers, GROUPS, PARTS, nz, rows, span), bf),
            pltpu.VMEM((layers, GROUPS, PARTS, nz, rows, span), bf),
            pltpu.VMEM((layers, GROUPS, PARTS, nz, rows, span), bf),
            pltpu.VMEM((GROUPS, rows, width), f32),
            pltpu.VMEM((GROUPS, rows, width), bf),
            pltpu.VMEM((GROUPS, rows, width), bf),
            dma((layers, 5)),
        ]
        + [dma((layers, GROUPS, nz))] * 4
        + [dma((layers, GROUPS, PARTS))] * 2
        + [dma((layers, GROUPS, PARTS, nz))] * 2,
        compiler_params=pltpu.CompilerParams(
            collective_id=0, has_side_effects=True, vmem_limit_bytes=60 * 2**20
        ),
    )(
        limits, targets[0], hist_keys[:, 0], hist_values[:, 0], w_query, w_gate, w_out, ln_gain
    )
    return refined[None]


def solution(mesh):
    return jax.shard_map(
        functools.partial(per_device, inner_size(mesh)),
        mesh=mesh,
        in_specs=(
            P(("groups", "users"), "hist", None),
            P(None, ("groups", "users"), "hist", None),
            P(None, ("groups", "users"), "hist", None),
            P(("groups", "users")),
            P(("groups", "users"), None),
            P(),
            P(),
            P(),
            P(),
        ),
        out_specs=P(("groups", "users"), "hist", None),
        check_vma=False,
    )
```

time: 91.1 us -> 89.4 us (0.981)
  Pallas kernels: 86.8 us -> 85.3 us
    pallas_call x1, Pallas kernels: 86.8 us -> 85.3 us  [per_device(): pl.pallas_call(functools.partial(kernel, ny, nz), out_shape=jax.ShapeDtyp...]
    reshape x0 -> x1, local copies, waits for them, and re-layouts: none -> 0.96 us  [per_device(): limits.reshape(n, GROUPS, rows).transpose(1, 0, 2)]
where the time goes in v2:
time: 89.4 us; the launch traced here: 89.2 us
  Pallas kernels  85.3 us (95%)
  local copies, waits for them, and re-layouts  2.62 us (3%)
    pallas_call x1, Pallas kernels, per_device(): pl.pallas_call(functools.partial(kernel, ny, nz), out_shape=jax.ShapeDtyp...  85.3 us

profile of v2, /device:TPU:0, one launch (start us, length us, event | category | flops | bytes accessed | tf_op | source)
XLA Modules:
  0.0 89.2 jit_solution(7187825424423673206)
XLA Ops:
  0.7 0.7 subtract_reduce_fusion
  1.4 0.1 sub.12
  1.4 1.0 %reshape.10.lim_ref = s32[2,256,1]{2,1,0:T(8,128)} reshape(s32[2,8,32]{2,1,0:T(8,128)S(1)} %bitcast.13) | data formatting | bytes 4096 | tf_op jit(solution)/shard_map/reshape | solution.py:266
  2.4 85.3 %shard_map.91 = bf16[64,1024]{1,0:T(8,128)(2,1)} custom-call(s32[2,256,1]{2,1,0:T(8,128)} %reshape.10.lim_ref, bf16[64,1024]{1,0:T(8,128)(2,1)} %bitcast.12, bf16[2,1536,1024]{2,1,0:T(8,128)(2,1)} %bitcast.9, bf16[2,1536,1024]{2,1,0:T(8,128)(2,1)} %bitcast.10, bf16[2,1024,1024]{2,1,0:T(8,128)(2,1)} %wq_ref.1, bf16[2,1024,1024]{2,1,0:T(8,128)(2,1)} %wg_ref.1, ...), custom_call_target="tpu_custom_call" | custom-call | tf_op jit(solution)/shard_map/pallas_call | solution.py:272
  87.7 1.6 %copy.17 = bf16[1,64,1024]{2,1,0:T(8,128)(2,1)} copy(bf16[1,64,1024]{2,1,0:T(8,128)(2,1)} %bitcast.11) | data formatting | bytes 262144
  (1 shorter events, 0.0 us)

commit v3 on v2

--- a/solution.py
+++ b/solution.py
@@ -12,7 +12,7 @@
 GROUPS = 2
 PARTS = 2
 CHUNK = 256
-UNROLL = 2
+UNROLL = 4
 MESH = pl.DeviceIdType.MESH
 
 
@@ -210,15 +210,19 @@
             for g in range(GROUPS):
                 if g == prev:
                     reduce(l - 1, prev, parts - 1)
+                    wait[3].wait()
+                    if prev > 0:
+                        gating(l, 0, prev)
+                        forward(l, 0)
                 finish(l - 1, g)
                 query(l, g, g + 1)
                 spread(l, g)
-            wait[3].wait()
-            gating(l, 0, GROUPS)
+            gating(l, prev, GROUPS)
         wait[1].wait()
         wait[2].wait()
         wait[4].wait()
-        forward(l, 0)
+        if l == 0 or GROUPS == 1:
+            forward(l, 0)
         arrive(l, 0)
         for g in range(GROUPS):
             for p in range(parts):

time: 89.4 us -> 86.2 us (0.964)
  Pallas kernels: 85.3 us -> 82 us
    pallas_call x1, Pallas kernels: 85.3 us -> 82 us  [per_device(): pl.pallas_call(functools.partial(kernel, ny, nz), out_shape=jax.ShapeDtyp...]
where the time goes in v3:
time: 86.2 us; the launch traced here: 86 us
  Pallas kernels  82 us (95%)
  local copies, waits for them, and re-layouts  2.62 us (3%)
    pallas_call x1, Pallas kernels, per_device(): pl.pallas_call(functools.partial(kernel, ny, nz), out_shape=jax.ShapeDtyp...  82 us

profile of v3, /device:TPU:0, one launch (start us, length us, event | category | flops | bytes accessed | tf_op | source)
XLA Modules:
  0.0 86.0 jit_solution(8428474263144052109)
XLA Ops:
  0.7 0.7 subtract_reduce_fusion
  1.4 0.1 sub.12
  1.4 1.0 %reshape.10.lim_ref = s32[2,256,1]{2,1,0:T(8,128)} reshape(s32[2,8,32]{2,1,0:T(8,128)S(1)} %bitcast.13) | data formatting | bytes 4096 | tf_op jit(solution)/shard_map/reshape | solution.py:270
  2.4 82.0 %shard_map.91 = bf16[64,1024]{1,0:T(8,128)(2,1)} custom-call(s32[2,256,1]{2,1,0:T(8,128)} %reshape.10.lim_ref, bf16[64,1024]{1,0:T(8,128)(2,1)} %bitcast.12, bf16[2,1536,1024]{2,1,0:T(8,128)(2,1)} %bitcast.9, bf16[2,1536,1024]{2,1,0:T(8,128)(2,1)} %bitcast.10, bf16[2,1024,1024]{2,1,0:T(8,128)(2,1)} %wq_ref.1, bf16[2,1024,1024]{2,1,0:T(8,128)(2,1)} %wg_ref.1, ...), custom_call_target="tpu_custom_call" | custom-call | tf_op jit(solution)/shard_map/pallas_call | solution.py:276
  84.5 1.6 %copy.17 = bf16[1,64,1024]{2,1,0:T(8,128)(2,1)} copy(bf16[1,64,1024]{2,1,0:T(8,128)(2,1)} %bitcast.11) | data formatting | bytes 262144
  (1 shorter events, 0.0 us)
